TPU v7x, 32 devices: a whole 2x2x4 slice. The times are simulated.
32 devices in a mesh: tok: 4 (over y, core), tp: 8 (over z, x).
Axes of the slice: x: 2, y: 2, z: 4, core: 2. Of those that a mesh axis runs over, the one named last changes fastest.
Arguments:
- residual: bfloat16 [1024, 16384], P('tok', 'tp')
- norm_gain: float32 [16384], replicated, may hold values from 0.5 to 1.5
- weight: bfloat16 [30720, 16384], P(('tok', 'tp')), may hold values from -6 to 6
- scale_codes: int32 [30720, 2], P(('tok', 'tp')), may hold values from 0 to 7
- zero_points: int32 [30720, 2], P(('tok', 'tp')), may hold values from 4 to 11
- panels: bfloat16 [256, 16384], P(None, ('tok', 'tp')), as said below
Outputs:
- gram: float32 [16384, 16384], P('tok', 'tp')
- quantized: bfloat16 [30720, 16384], P('tok', 'tp')
Inputs may be any that keep to these rules, and one draw needn't show every extreme that they name: Row j of panels is row j of an upper-triangular factor: entries left of column j are zero and panels[j, j] lies in [0.5, 1.5].
All inputs are finite; a program needn't handle non-finite values.
Results may differ from a plain program's by a relative error of at most 0.0085.
Values may be sent and summed in bfloat16 or wider, within the bound.
A program may use at most 384 MiB of HBM per device.

v0:
```python
import math

import jax
import jax.numpy as jnp
from jax import lax
from jax.sharding import PartitionSpec as P

BLOCK = 128
BLOCKS = 2


EPS = 1e-05
SOFTNESS = 0.9
FULL_TURN = 2.0 * math.pi
HIGHEST = lax.Precision.HIGHEST


def spread(x, axis, root):
    mine = lax.axis_index(axis) == root
    return lax.psum(jnp.where(mine, x, jnp.zeros_like(x)), axis)


def dequantize(column, scale_row, zero_row):
    shifted = column / scale_row + zero_row
    softened = shifted - SOFTNESS * jnp.sin(FULL_TURN * shifted) / FULL_TURN
    return scale_row * (jnp.clip(softened, 0.0, 15.0) - zero_row)


def block_errors(block_cols, diagonal, scale_row, zero_row):
    row_count = block_cols.shape[0]
    block_width = block_cols.shape[1]
    lane_ids = lax.iota(jnp.int32, 8)
    wide_ids = lax.iota(jnp.int32, block_width)

    def sub_step(step_index, carried):
        block_now, errors = carried
        sub_first = step_index * 8
        sub_cols = lax.dynamic_slice_in_dim(block_now, sub_first, 8, 1)
        sub_panel = lax.dynamic_slice_in_dim(diagonal, sub_first, 8, 0)
        local_pivots = lax.dynamic_slice_in_dim(sub_panel, sub_first, 8, 1)
        collected = []
        for i in range(8):
            column_now = sub_cols[:, i]
            restored = dequantize(column_now, scale_row, zero_row)
            error_now = (column_now - restored) / local_pivots[i, i]
            sub_cols = (
                sub_cols
                - error_now[:, None] * jnp.where(lane_ids > i, local_pivots[i], 0.0)[None, :]
            )
            sub_cols = jnp.where((lane_ids == i)[None, :], restored[:, None], sub_cols)
            collected.append(error_now)
        sub_errors = jnp.stack(collected, axis=1)
        spill_over = jnp.dot(sub_errors, sub_panel, precision=HIGHEST)
        block_now = jnp.where(
            (wide_ids >= sub_first + 8)[None, :], block_now - spill_over, block_now
        )
        block_now = lax.dynamic_update_slice_in_dim(block_now, sub_cols, sub_first, 1)
        errors = lax.dynamic_update_slice_in_dim(errors, sub_errors, sub_first, 1)
        return (block_now, errors)

    start_state = (block_cols, jnp.zeros((row_count, block_width), jnp.float32))
    return lax.fori_loop(0, block_width // 8, sub_step, start_state)


def on_device(residual, norm_gain, weight, scale_codes, zero_points, panels):
    tok_local, feat_local = residual.shape
    tp_count = lax.axis_size("tp")
    tok_count = lax.axis_size("tok")
    feat_total = feat_local * tp_count
    tp_place = lax.axis_index("tp")
    local_rows = residual.astype(jnp.float32)
    row_sums = lax.psum(jnp.sum(local_rows * local_rows, axis=1), "tp")
    gain_own = lax.dynamic_slice_in_dim(norm_gain, tp_place * feat_local, feat_local, 0)
    x_own = (
        local_rows * lax.rsqrt(row_sums[:, None] / feat_total + EPS) * gain_own[None, :]
    ).astype(jnp.bfloat16)
    x_full = lax.all_gather(x_own, "tp", axis=1, tiled=True)
    gram_sum = lax.psum_scatter(
        lax.dot_general(
            x_full, x_own, (((0,), (0,)), ((), ())), preferred_element_type=jnp.float32
        ).astype(jnp.bfloat16),
        "tok",
        scatter_dimension=0,
        tiled=True,
    ).astype(jnp.float32)
    gram = gram_sum / (tok_local * tok_count)
    shard_cols = panels.shape[1]
    working = weight.astype(jnp.float32)
    column = lax.iota(jnp.int32, feat_total)
    for k in range(BLOCKS):
        block_start = k * BLOCK
        scale_row = jnp.exp2(scale_codes[:, k].astype(jnp.float32) * 0.5 - 3.0)
        zero_row = zero_points[:, k].astype(jnp.float32)
        root_index = block_start // shard_cols
        offset_cols = block_start - root_index * shard_cols
        own_block = panels[block_start : block_start + BLOCK, offset_cols : offset_cols + BLOCK]
        diagonal = spread(own_block, ("tok", "tp"), root_index).astype(jnp.float32)
        block_cols, errors = block_errors(
            working[:, block_start : block_start + BLOCK], diagonal, scale_row, zero_row
        )
        correction = jnp.dot(
            errors,
            lax.all_gather(
                panels[block_start : block_start + BLOCK], ("tok", "tp"), axis=1, tiled=True
            ).astype(jnp.float32),
            precision=HIGHEST,
        )
        working = jnp.where((column >= block_start + BLOCK)[None, :], working - correction, working)
        working = lax.dynamic_update_slice_in_dim(working, block_cols, block_start, 1)
    quantized = lax.all_to_all(
        working.astype(jnp.bfloat16), "tp", split_axis=1, concat_axis=0, tiled=True
    )
    return (gram, quantized)


def solution(mesh):
    in_specs = (
        P("tok", "tp"),
        P(),
        P(("tok", "tp"), None),
        P(("tok", "tp"), None),
        P(("tok", "tp"), None),
        P(None, ("tok", "tp")),
    )
    out_specs = (P("tok", "tp"), P("tok", "tp"))
    return jax.shard_map(
        on_device, mesh=mesh, in_specs=in_specs, out_specs=out_specs, check_vma=False
    )
```

profile of v0, /device:TPU:1, one launch (start us, length us, event | category | flops | bytes accessed | tf_op | source)
XLA Modules:
  0.0 1459.3 jit_solution(8556736024828552044)
XLA Ops:
  12.7 18.7 %psum.21 = f32[256]{0:T(256)S(1)} all-reduce(f32[256]{0:T(256)S(1)} %fusion.62), channel_id=1, replica_groups=mesh['tok'=4,'tp'=8] {'tp'}, use_global_device_ids=true, to_apply=%region_1.0 | all-reduce | flops 256 | bytes 2048 | tf_op jit(solution)/shard_map/psum | solution.py:72
  37.4 100.4 %all-reduce.4.cloned.1.call-done = (bf16[128,128]{1,0:T(8,128)(2,1)}, bf16[128,128]{1,0:T(8,128)(2,1)}) async-done(((bf16[128,128]{1,0:T(8,128)(2,1)}, bf16[128,128]{1,0:T(8,128)(2,1)}), (bf16[128,128]{1,0:T(8,128)(2,1)}, bf16[128,128]{1,0:T(8,128)(2,1)})) %all-reduce.4.cloned.1.call-update) | async-done | bytes 65552 | tf_op jit(solution)/shard_map/psum | solution.py:20
  138.6 221.0 %while.40 = (s32[]{:T(128)}, f32[960,128]{0,1:T(8,128)S(1)}, f32[960,128]{0,1:T(8,128)S(1)}, f32[960]{0:T(1024)S(1)}, f32[960]{0:T(1024)S(1)}, /*index=5*/f32[12...) while((s32[]{:T(128)}, f32[960,128]{0,1:T(8,128)S(1)}, ...), condition=%wide.region_5.6_spmd.clone.clone, body=%wide.region_4.5_spmd.clone.clone.sunk | while | flops 12948808 | bytes 4160943 | solution.py:62
  160.8 4.5 dynamic_update_slice.69
  174.6 4.5 dynamic_update_slice.69
  188.5 4.5 dynamic_update_slice.69
  202.4 4.5 dynamic_update_slice.69
  216.2 4.5 dynamic_update_slice.69
  257.8 4.5 dynamic_update_slice.69
  285.5 4.5 dynamic_update_slice.69
  299.4 4.5 dynamic_update_slice.69
  327.1 4.5 dynamic_update_slice.69
  341.0 4.5 dynamic_update_slice.69
  360.5 42.3 %subtract_select_fusion.17 = f32[960,16384]{1,0:T(8,128)} fusion(f32[960,128]{0,1:T(8,128)S(1)} %get-tuple-element.574, bf16[128,16384]{1,0:T(8,128)(2,1)} %all-gather.6.cloned.1.call-done, pred[16384]{0:T(1024)(128)(4,1)S(1)} %iota_compare_fusion.34, bf16[960,16384]{1,0:T(8,128)(2,1)} %param.12), kind=kOutput, calls=%fused_computation.145 | convolution fusion | flops 24206376960 | bytes 99074048 | tf_op jit(solution)/shard_map/dot_general | solution.py:101
  405.0 29.4 %convolution_convert_fusion = bf16[16384,2048]{1,0:T(8,128)(2,1)} fusion(bf16[256,16384]{1,0:T(8,128)(2,1)} %all-gather.4.cloned.1.call-done, bf16[256,2048]{1,0:T(8,128)(2,1)S(1)} %copy-done), kind=kOutput, calls=%fused_computation.146 | convolution fusion | flops 17213423616 | bytes 76546048 | tf_op jit(solution)/shard_map/dot_general | solution.py:79
  434.5 226.1 %while.41 = (s32[]{:T(128)}, f32[960,128]{0,1:T(8,128)S(1)}, f32[960,128]{0,1:T(8,128)S(1)}, f32[960]{0:T(1024)S(1)}, f32[960]{0:T(1024)S(1)}, /*index=5*/f32[12...) while((s32[]{:T(128)}, f32[960,128]{0,1:T(8,128)S(1)}, ...), condition=%wide.region_8.9_spmd.clone.clone, body=%wide.region_7.8_spmd.clone.clone.sunk | while | flops 12948808 | bytes 4160943 | solution.py:62
  457.5 4.5 dynamic_update_slice.71
  471.7 4.5 dynamic_update_slice.71
  500.1 4.5 dynamic_update_slice.71
  528.4 4.5 dynamic_update_slice.71
  542.6 4.5 dynamic_update_slice.71
  556.7 4.5 dynamic_update_slice.71
  599.2 4.5 dynamic_update_slice.71
  613.4 4.5 dynamic_update_slice.71
  627.6 4.5 dynamic_update_slice.71
  641.7 4.5 dynamic_update_slice.71
  655.9 4.5 dynamic_update_slice.71
  660.8 41.6 %subtract_select_fusion.16 = bf16[960,16384]{1,0:T(8,128)(2,1)} fusion(f32[960,16384]{1,0:T(8,128)} %constant_dynamic-update-slice_fusion.3, f32[960,128]{0,1:T(8,128)S(1)} %get-tuple-element.576, bf16[128,16384]{1,0:T(8,128)(2,1)} %all-gather.8.cloned.1.call-done, pred[16384]{0:T(1024)(128)(4,1)S(1)} %iota_compare_fusion.35), kind=kOutput, calls=%fused_computation.144 | convolution fusion | flops 24190648320 | bytes 99074048 | tf_op jit(solution)/shard_map/dot_general | solution.py:101
  703.2 21.7 %copy.170 = bf16[120,8,8,2048]{3,2,0,1:T(8,128)(2,1)} copy(bf16[120,8,8,2048]{3,2,1,0:T(8,128)(2,1)} %bitcast.316) | data formatting | bytes 62914560 | tf_op jit(solution)/shard_map/all_to_all | solution.py:110
  724.9 687.8 %all_to_all.19 = bf16[960,8,2048]{2,0,1:T(8,128)(2,1)} all-to-all(bf16[960,8,2048]{2,0,1:T(8,128)(2,1)} %bitcast.318), channel_id=1, replica_groups=mesh['tok'=4,'tp'=8] {'tp'}, dimensions={1} | all-to-all | bytes 62914560 | tf_op jit(solution)/shard_map/all_to_all | solution.py:110
  1412.6 18.8 %convert_multiply_fusion = f32[4096,2048]{1,0:T(8,128)} fusion(bf16[4096,2048]{1,0:T(8,128)(2,1)} %reduce-scatter.4.cloned.1.call-done), kind=kLoop, calls=%fused_computation.147 | loop fusion | flops 16777216 | bytes 50331648 | tf_op jit(solution)/shard_map/div | solution.py:86
  1431.4 21.3 %copy.210 = bf16[7680,2048]{1,0:T(8,128)(2,1)} copy(bf16[7680,2048]{1,0:T(8,128)(2,1)} %bitcast.317) | data formatting | bytes 62914560
  (1137 shorter events, 363.9 us)
Async XLA Ops:
  7.2 130.6 %all-reduce.4.cloned.1.call-start = ((), (), s32[]{:S(2)}) async-start(), calls=%async_computation.6 | async-start | bytes 131072 | tf_op jit(solution)/shard_map/psum | solution.py:20
  8.7 351.9 %all-gather.6.cloned.1.call-start = ((), (), s32[]{:S(2)}) async-start(), calls=%async_computation.3 | async-start | bytes 4325376 | tf_op jit(solution)/shard_map/all_gather | solution.py:103
  10.4 394.6 %all-gather.4.cloned.1.call-start = ((), (), s32[]{:S(2)}) async-start(), calls=%async_computation.2 | async-start | bytes 9437184 | tf_op jit(solution)/shard_map/all_gather | solution.py:77
  33.9 626.9 %all-gather.8.cloned.1.call-start = ((), (), s32[]{:S(2)}) async-start(), calls=%async_computation.4 | async-start | bytes 4325376 | tf_op jit(solution)/shard_map/all_gather | solution.py:103
  34.5 1378.1 %reduce-scatter.4.cloned.1.call-start = ((), (), s32[]{:S(2)}) async-start(), calls=%async_computation.5 | async-start | bytes 83886080
  360.5 44.5 %copy-start = (bf16[256,2048]{1,0:T(8,128)(2,1)S(1)}, bf16[256,2048]{1,0:T(8,128)(2,1)}, u32[]{:S(2)}) copy-start(bf16[256,2048]{1,0:T(8,128)(2,1)} %fusion.64) | copy-start | bytes 3145732
Sparse Core Ops, SparseCore 0:
  13.7 124.0 all-reduce.3
  140.6 62.9 all-gather.5
  206.4 121.5 all-gather.3
  331.3 62.2 all-gather.7
  434.5 445.9 reduce-scatter.3
where the time goes:
time: 1460 us
  blocking collectives  706 us (48%)
  other arithmetic  251 us (17%)
  local copies, waits for them, and re-layouts  237 us (16%)
  matrix products  144 us (10%)
  waiting for transfers between devices  101 us (7%)
    all_to_all x1, blocking collectives, on_device(): lax.all_to_all(working.astype(jnp.bfloat16), 'tp', split_axis=1, concat_a...  688 us
    div x256, other arithmetic, sub_step(): error_now = (column_now - restored) / local_pivots[i, i]  197 us
    dynamic_update_slice x32, local copies, waits for them, and re-layouts, sub_step(): lax.dynamic_update_slice_in_dim(block_now, sub_cols, sub_first, 1)  142 us
    psum x1, waiting for transfers between devices, spread(): return lax.psum(jnp.where(mine, x, jnp.zeros_like(x)), axis)  100 us
    dot_general x2, matrix products, on_device(): jnp.dot(errors, lax.all_gather(panels[block_start:block_start + BLOCK], (...  84 us
    dot_general x32, matrix products, sub_step(): spill_over = jnp.dot(sub_errors, sub_panel, precision=HIGHEST)  30.6 us
    dot_general x1, matrix products, on_device(): lax.dot_general(x_full, x_own, (((0,), (0,)), ((), ())), preferred_elemen...  29.4 us
  transfers between devices with their start and end apart: 5, of which 1 were waited for; matrix products, arithmetic and copies ran while one was open for 40% of the time, Pallas kernels for 0%

commit v1 on v0

--- a/solution.py
+++ b/solution.py
@@ -4,6 +4,7 @@
 import jax.numpy as jnp
 from jax import lax
 from jax.sharding import PartitionSpec as P
+
 
 BLOCK = 128
 BLOCKS = 2
@@ -13,11 +14,6 @@
 SOFTNESS = 0.9
 FULL_TURN = 2.0 * math.pi
 HIGHEST = lax.Precision.HIGHEST
-
-
-def spread(x, axis, root):
-    mine = lax.axis_index(axis) == root
-    return lax.psum(jnp.where(mine, x, jnp.zeros_like(x)), axis)
 
 
 def dequantize(column, scale_row, zero_row):
@@ -62,54 +58,120 @@
     return lax.fori_loop(0, block_width // 8, sub_step, start_state)
 
 
+def exchange(array, axis, step):
+    count = lax.axis_size(axis)
+    return lax.ppermute(array, axis, [(i, i ^ step) for i in range(count)])
+
+
+def far_first(count):
+    return sorted(range(1, count), reverse=True)
+
+
+def panel_columns(panels):
+    tok_count = lax.axis_size("tok")
+    tp_count = lax.axis_size("tp")
+    tok_place = lax.axis_index("tok")
+    pieces = []
+    for r in range(tok_count):
+        pairs = []
+        for t in range(tok_count):
+            for p in range(tp_count):
+                source = tok_count * p + (t + r) % tok_count
+                pairs.append((source, t * tp_count + p))
+        pieces.append(lax.ppermute(panels, ("tok", "tp"), pairs))
+    stacked = jnp.stack(pieces)
+    ordered = [
+        lax.dynamic_index_in_dim(stacked, (i - tok_place) % tok_count, 0, keepdims=False)
+        for i in range(tok_count)
+    ]
+    return jnp.concatenate(ordered, axis=1)
+
+
 def on_device(residual, norm_gain, weight, scale_codes, zero_points, panels):
     tok_local, feat_local = residual.shape
     tp_count = lax.axis_size("tp")
     tok_count = lax.axis_size("tok")
     feat_total = feat_local * tp_count
     tp_place = lax.axis_index("tp")
+    tok_place = lax.axis_index("tok")
+    row_count = weight.shape[0]
+
+    def columns_of(place):
+        return lax.dynamic_slice_in_dim(weight, place * feat_local, feat_local, 1)
+
+    chunks = {}
+    for s in far_first(tp_count):
+        chunks[s] = exchange(columns_of(tp_place ^ s), "tp", s)
+    chunks[0] = columns_of(tp_place)
+
+    shard_cols = panels.shape[1]
+    corner_parts = []
+    for k in range(BLOCKS):
+        root_index = k * BLOCK // shard_cols
+        offset_cols = k * BLOCK - root_index * shard_cols
+        corner_parts.append(
+            jnp.where(
+                lax.axis_index(("tok", "tp")) == root_index,
+                panels[:, offset_cols : offset_cols + BLOCK],
+                0,
+            )
+        )
+    corner = lax.psum(jnp.concatenate(corner_parts, axis=1), ("tok", "tp")).astype(jnp.float32)
+
     local_rows = residual.astype(jnp.float32)
     row_sums = lax.psum(jnp.sum(local_rows * local_rows, axis=1), "tp")
     gain_own = lax.dynamic_slice_in_dim(norm_gain, tp_place * feat_local, feat_local, 0)
     x_own = (
         local_rows * lax.rsqrt(row_sums[:, None] / feat_total + EPS) * gain_own[None, :]
     ).astype(jnp.bfloat16)
+    working = weight[:, : BLOCKS * BLOCK].astype(jnp.float32)
+    working, x_own = lax.optimization_barrier((working, x_own))
     x_full = lax.all_gather(x_own, "tp", axis=1, tiled=True)
-    gram_sum = lax.psum_scatter(
-        lax.dot_general(
-            x_full, x_own, (((0,), (0,)), ((), ())), preferred_element_type=jnp.float32
-        ).astype(jnp.bfloat16),
-        "tok",
-        scatter_dimension=0,
-        tiled=True,
-    ).astype(jnp.float32)
-    gram = gram_sum / (tok_local * tok_count)
-    shard_cols = panels.shape[1]
-    working = weight.astype(jnp.float32)
-    column = lax.iota(jnp.int32, feat_total)
+    all_errors = []
     for k in range(BLOCKS):
-        block_start = k * BLOCK
+        if k == 1:
+            all_errors[0], x_full = lax.optimization_barrier((all_errors[0], x_full))
+        first = k * BLOCK
         scale_row = jnp.exp2(scale_codes[:, k].astype(jnp.float32) * 0.5 - 3.0)
         zero_row = zero_points[:, k].astype(jnp.float32)
-        root_index = block_start // shard_cols
-        offset_cols = block_start - root_index * shard_cols
-        own_block = panels[block_start : block_start + BLOCK, offset_cols : offset_cols + BLOCK]
-        diagonal = spread(own_block, ("tok", "tp"), root_index).astype(jnp.float32)
-        block_cols, errors = block_errors(
-            working[:, block_start : block_start + BLOCK], diagonal, scale_row, zero_row
+        block_cols = working[:, first : first + BLOCK]
+        for before in range(k):
+            block_cols = block_cols - jnp.dot(
+                all_errors[before],
+                corner[before * BLOCK : (before + 1) * BLOCK, first : first + BLOCK],
+                precision=HIGHEST,
+            )
+        _, errors = block_errors(
+            block_cols, corner[first : first + BLOCK, first : first + BLOCK], scale_row, zero_row
         )
-        correction = jnp.dot(
-            errors,
-            lax.all_gather(
-                panels[block_start : block_start + BLOCK], ("tok", "tp"), axis=1, tiled=True
-            ).astype(jnp.float32),
-            precision=HIGHEST,
+        all_errors.append(errors)
+    own_errors = jnp.concatenate(all_errors, axis=1).astype(jnp.bfloat16)
+    errors_of = lax.all_gather(own_errors, "tp", axis=0)
+    own_panels = panel_columns(panels)
+
+    gram_rows = feat_total // tok_count
+    left, right = [], []
+    for s in range(tok_count):
+        slab = lax.dynamic_slice_in_dim(x_full, (tok_place ^ s) * gram_rows, gram_rows, 1)
+        left.append(exchange(slab, "tok", s) if s else slab)
+        right.append(exchange(x_own, "tok", s) if s else x_own)
+    gram = lax.dot_general(
+        jnp.concatenate(left, axis=0),
+        jnp.concatenate(right, axis=0),
+        (((0,), (0,)), ((), ())),
+        preferred_element_type=jnp.float32,
+    ) / (tok_local * tok_count)
+
+    quantized = jnp.zeros((row_count * tp_count, feat_local), jnp.bfloat16)
+    for s in sorted(range(tp_count), key=lambda s: (s != 0, s)):
+        source = tp_place ^ s
+        moved = jnp.dot(
+            lax.dynamic_index_in_dim(errors_of, source, 0, keepdims=False),
+            own_panels,
+            preferred_element_type=jnp.float32,
         )
-        working = jnp.where((column >= block_start + BLOCK)[None, :], working - correction, working)
-        working = lax.dynamic_update_slice_in_dim(working, block_cols, block_start, 1)
-    quantized = lax.all_to_all(
-        working.astype(jnp.bfloat16), "tp", split_axis=1, concat_axis=0, tiled=True
-    )
+        rows_now = (chunks[s].astype(jnp.float32) - moved).astype(jnp.bfloat16)
+        quantized = lax.dynamic_update_slice_in_dim(quantized, rows_now, source * row_count, 0)
     return (gram, quantized)
 
 
@@ -123,6 +185,5 @@
         P(None, ("tok", "tp")),
     )
     out_specs = (P("tok", "tp"), P("tok", "tp"))
-    return jax.shard_map(
-        on_device, mesh=mesh, in_specs=in_specs, out_specs=out_specs, check_vma=False
-    )
+
+    return jax.shard_map(on_device, mesh=mesh, in_specs=in_specs, out_specs=out_specs, check_vma=False)

time: 1460 us -> 1430 us (0.979)
  the two profiles are of different devices: /device:TPU:1 before, /device:TPU:9 now
where the time goes in v1:
time: 1430 us
  waiting for transfers between devices  775 us (54%)
  other arithmetic  233 us (16%)
  local copies, waits for them, and re-layouts  226 us (16%)
  matrix products  100 us (7%)
  blocking collectives  43.8 us (3%)
  starting transfers between devices  28.3 us (2%)
  between operations  15.8 us (1%)
    all_gather x1, waiting for transfers between devices, on_device(): errors_of = lax.all_gather(own_errors, 'tp', axis=0)  366 us
    ppermute x13, waiting for transfers between devices, exchange(): return lax.ppermute(array, axis, [(i, i ^ step) for i in range(count)])  277 us
    div x256, other arithmetic, sub_step(): error_now = (column_now - restored) / local_pivots[i, i]  198 us
    dynamic_update_slice x32, local copies, waits for them, and re-layouts, sub_step(): lax.dynamic_update_slice_in_dim(block_now, sub_cols, sub_first, 1)  142 us
    psum x1, waiting for transfers between devices, on_device(): lax.psum(jnp.concatenate(corner_parts, axis=1), ('tok', 'tp'))  132 us
    psum x1, blocking collectives, on_device(): row_sums = lax.psum(jnp.sum(local_rows * local_rows, axis=1), 'tp')  43.8 us
    dot_general x8, matrix products, on_device(): jnp.dot(lax.dynamic_index_in_dim(errors_of, source, 0, keepdims=False), o...  42.2 us
    dot_general x32, matrix products, sub_step(): spill_over = jnp.dot(sub_errors, sub_panel, precision=HIGHEST)  30.6 us
  transfers between devices with their start and end apart: 20, of which 7 were waited for; matrix products, arithmetic and copies ran while one was open for 39% of the time, Pallas kernels for 0%

profile of v1, /device:TPU:9, one launch (start us, length us, event | category | flops | bytes accessed | tf_op | source)
XLA Modules:
  0.0 1428.2 jit_solution(2348529837407172118)
XLA Ops:
  21.5 43.8 %psum.14 = f32[256]{0:T(256)S(1)} all-reduce(f32[256]{0:T(256)S(1)} %fusion.84), channel_id=1, replica_groups=mesh['tok'=4,'tp'=8] {'tp'}, use_global_device_ids=true, to_apply=%region_1.2 | all-reduce | flops 256 | bytes 2048 | tf_op jit(solution)/shard_map/psum | solution.py:122
  74.0 19.2 %constant_dynamic-slice_fusion.2 = (bf16[960,2048]{1,0:T(8,128)(2,1)}, bf16[960,2048]{1,0:T(8,128)(2,1)}, bf16[960,2048]{1,0:T(8,128)(2,1)}, bf16[960,2048]{1,0:...) fusion(bf16[960,16384]{1,0:T(8,128)(2,1)} %param.12, ...), kind=kLoop, calls=%fused_computation.222 | loop fusion | bytes 55050268 | tf_op jit(solution)/shard_map/dynamic_slice | solution.py:100
  93.3 132.5 %all-reduce.2.cloned.1.call-done = bf16[256,256]{1,0:T(8,128)(2,1)} async-done(((bf16[256,256]{1,0:T(8,128)(2,1)}), bf16[256,256]{1,0:T(8,128)(2,1)}) %all-reduce.2.cloned.1.call-update) | async-done | bytes 131088 | tf_op jit(solution)/shard_map/psum | solution.py:119
  226.6 223.1 %while.40 = (s32[]{:T(128)}, f32[960,128]{0,1:T(8,128)S(1)}, f32[960,128]{0,1:T(8,128)S(1)}, f32[960]{0:T(1024)S(1)}, f32[960]{0:T(1024)S(1)}, /*index=5*/f32[12...) while((s32[]{:T(128)}, f32[960,128]{0,1:T(8,128)S(1)}, ...), condition=%wide.region_4.5_spmd.clone.clone, body=%wide.region_3.4_spmd.clone.clone.sunk | while | flops 12948808 | bytes 4160943 | solution.py:58
  263.1 4.5 dynamic_update_slice.99
  291.1 4.5 dynamic_update_slice.99
  319.1 4.5 dynamic_update_slice.99
  333.1 4.5 dynamic_update_slice.99
  347.1 4.5 dynamic_update_slice.99
  361.0 4.5 dynamic_update_slice.99
  375.0 4.5 dynamic_update_slice.99
  389.0 4.5 dynamic_update_slice.99
  417.0 4.5 dynamic_update_slice.99
  445.0 4.5 dynamic_update_slice.99
  457.4 224.4 %while.41 = (s32[]{:T(128)}, f32[960,128]{0,1:T(8,128)S(1)}, bf16[960,128]{0,1:T(8,128)(2,1)S(1)}, f32[960]{0:T(1024)S(1)}, f32[960]{0:T(1024)S(1)}, /*index=5*/...) while((s32[]{:T(128)}, f32[960,128]{0,1:T(8,128)S(1)}, ...), condition=%wide.region_6.7_spmd.clone.clone, body=%wide.region_5.6_spmd.clone.clone.sunk | while | flops 12948808 | bytes 4160943 | solution.py:58
  683.1 6.4 constant_dynamic-slice_fusion.10
  697.5 39.9 %collective-permute-done.1 = bf16[256,4096]{1,0:T(8,128)(2,1)} collective-permute-done((bf16[256,4096]{1,0:T(8,128)(2,1)}, bf16[256,4096]{1,0:T(8,128)(2,1)}, u32[]{:S(2)}, u32[]{:S(2)}) %collective-permute-start.1) | collective-permute-done | bytes 2097184 | tf_op jit(solution)/shard_map/ppermute | solution.py:63
  737.9 45.1 %collective-permute-done.2 = bf16[256,4096]{1,0:T(8,128)(2,1)} collective-permute-done((bf16[256,4096]{1,0:T(8,128)(2,1)}, bf16[256,4096]{1,0:T(8,128)(2,1)}, u32[]{:S(2)}, u32[]{:S(2)}) %collective-permute-start.2) | collective-permute-done | bytes 2097184 | tf_op jit(solution)/shard_map/ppermute | solution.py:63
  784.0 25.9 %convolution_multiply_fusion = f32[4096,2048]{1,0:T(8,128)} fusion(bf16[256,4096]{1,0:T(8,128)(2,1)} %collective-permute-done.2, bf16[256,4096]{1,0:T(8,128)(2,1)} %collective-permute-done.1, bf16[256,4096]{1,0:T(8,128)(2,1)} %collective-permute-done, bf16[256,4096]{1,0:T(8,128)(2,1)S(1)} %get-tuple-element.799, ...), kind=kOutput, calls=%fused_computation.144 | convolution fusion | flops 17238589440 | bytes 46137344 | tf_op jit(solution)/shard_map/dot_general | solution.py:158
  809.9 365.5 %all-gather.5.cloned.1.call-done = bf16[8,960,256]{2,1,0:T(8,128)(2,1)} async-done(((bf16[1,960,256]{2,1,0:T(8,128)(2,1)}), bf16[8,960,256]{2,1,0:T(8,128)(2,1)}) %all-gather.5.cloned.1.call-update) | async-done | bytes 3932176 | tf_op jit(solution)/shard_map/all_gather | solution.py:149
  1175.4 11.0 broadcast_in_dim.971
  1186.4 5.3 fusion.83
  1191.7 5.3 fusion.76
  1196.9 5.3 fusion.77
  1202.2 5.3 fusion.78
  1207.5 5.3 fusion.79
  1212.7 31.0 %collective-permute-done.14 = bf16[960,2048]{1,0:T(8,128)(2,1)} collective-permute-done((bf16[960,2048]{1,0:T(8,128)(2,1)}, bf16[960,2048]{1,0:T(8,128)(2,1)}, u32[]{:S(2)}, u32[]{:S(2)}) %collective-permute-start.14) | collective-permute-done | bytes 3932192 | tf_op jit(solution)/shard_map/ppermute | solution.py:63
  1243.7 5.3 fusion.80
  1249.0 81.3 %collective-permute-done.15 = bf16[960,2048]{1,0:T(8,128)(2,1)} collective-permute-done((bf16[960,2048]{1,0:T(8,128)(2,1)}, bf16[960,2048]{1,0:T(8,128)(2,1)}, u32[]{:S(2)}, u32[]{:S(2)}) %collective-permute-start.15) | collective-permute-done | bytes 3932192 | tf_op jit(solution)/shard_map/ppermute | solution.py:63
  1330.3 5.3 fusion.81
  1335.6 79.9 %collective-permute-done.16 = bf16[960,2048]{1,0:T(8,128)(2,1)} collective-permute-done((bf16[960,2048]{1,0:T(8,128)(2,1)}, bf16[960,2048]{1,0:T(8,128)(2,1)}, u32[]{:S(2)}, u32[]{:S(2)}) %collective-permute-start.16) | collective-permute-done | bytes 3932192 | tf_op jit(solution)/shard_map/ppermute | solution.py:63
  1415.4 5.3 fusion.82
  (1175 shorter events, 438.8 us)
Async XLA Ops:
  8.0 217.7 %all-reduce.2.cloned.1.call-start = ((), (), s32[]{:S(2)}) async-start(), calls=%async_computation | async-start | bytes 262144 | tf_op jit(solution)/shard_map/psum | solution.py:119
  8.0 443.6 %collective-permute-start.9 = (bf16[256,512]{1,0:T(8,128)(2,1)}, bf16[256,512]{1,0:T(8,128)(2,1)S(1)}, u32[]{:S(2)}, u32[]{:S(2)}) collective-permute-start(bf16[256,512]{1,0:T(8,128)(2,1)} %param.15), channel_id=1, source_target_pairs={{3,0},{7,1},{11,2},{15,3},{19,4},{23,5},{27,6},{31,7},{0,8},{4,9},... | collective-permute-start | bytes 786440 | tf_op jit(solution)/shard_map/ppermute | solution.py:81
  11.2 441.7 %collective-permute-start.6 = (bf16[256,512]{1,0:T(8,128)(2,1)}, bf16[256,512]{1,0:T(8,128)(2,1)S(1)}, u32[]{:S(2)}, u32[]{:S(2)}) collective-permute-start(bf16[256,512]{1,0:T(8,128)(2,1)} %param.15), channel_id=1, source_target_pairs={{0,0},{4,1},{8,2},{12,3},{16,4},{20,5},{24,6},{28,7},{1,8},{5,9},{... | collective-permute-start | bytes 786440 | tf_op jit(solution)/shard_map/ppermute | solution.py:81
  14.7 441.3 %collective-permute-start.7 = (bf16[256,512]{1,0:T(8,128)(2,1)}, bf16[256,512]{1,0:T(8,128)(2,1)}, u32[]{:S(2)}, u32[]{:S(2)}) collective-permute-start(bf16[256,512]{1,0:T(8,128)(2,1)} %param.15), channel_id=1, source_target_pairs={{1,0},{5,1},{9,2},{13,3},{17,4},{21,5},{25,6},{29,7},{2,8},{6,9},{... | collective-permute-start | bytes 786440 | tf_op jit(solution)/shard_map/ppermute | solution.py:81
  18.3 438.9 %collective-permute-start.8 = (bf16[256,512]{1,0:T(8,128)(2,1)}, bf16[256,512]{1,0:T(8,128)(2,1)}, u32[]{:S(2)}, u32[]{:S(2)}) collective-permute-start(bf16[256,512]{1,0:T(8,128)(2,1)} %param.15), channel_id=1, source_target_pairs={{2,0},{6,1},{10,2},{14,3},{18,4},{22,5},{26,6},{30,7},{3,8},{7,9},... | collective-permute-start | bytes 786440 | tf_op jit(solution)/shard_map/ppermute | solution.py:81
  19.9 429.9 %all-gather.3.cloned.1.call-start = ((), (), s32[]{:S(2)}) async-start(), calls=%async_computation.1 | async-start | bytes 9437184 | tf_op jit(solution)/shard_map/all_gather | solution.py:129
  19.9 54.0 %copy-start.1 = (s32[960,2]{0,1:T(2,128)S(1)}, s32[960,2]{0,1:T(2,128)}, u32[]{:S(2)}) copy-start(s32[960,2]{0,1:T(2,128)} %param.13) | copy-start | bytes 23044
  19.9 54.0 %copy-start.2 = (s32[960,2]{0,1:T(2,128)S(1)}, s32[960,2]{0,1:T(2,128)}, u32[]{:S(2)}) copy-start(s32[960,2]{0,1:T(2,128)} %param.14) | copy-start | bytes 23044
  69.6 4.1 copy-start
  69.6 619.9 %collective-permute-start.3 = (bf16[256,2048]{1,0:T(8,128)(2,1)}, bf16[256,2048]{1,0:T(8,128)(2,1)}, u32[]{:S(2)}, u32[]{:S(2)}) collective-permute-start(bf16[256,2048]{1,0:T(8,128)(2,1)} %fusion.86), channel_id=1, source_target_pairs={{0,8},{8,0},{16,24},{24,16},{1,9},{9,1},{17,25},{25,17},{2,10},{10... | collective-permute-start | bytes 3145736 | tf_op jit(solution)/shard_map/ppermute | solution.py:63
  73.5 1101.9 %all-gather.5.cloned.1.call-start = ((), (), s32[]{:S(2)}) async-start(), calls=%async_computation.2 | async-start | bytes 4423680 | tf_op jit(solution)/shard_map/all_gather | solution.py:149
  451.6 238.4 %collective-permute-start.4 = (bf16[256,2048]{1,0:T(8,128)(2,1)}, bf16[256,2048]{1,0:T(8,128)(2,1)}, u32[]{:S(2)}, u32[]{:S(2)}) collective-permute-start(bf16[256,2048]{1,0:T(8,128)(2,1)} %fusion.86), channel_id=1, source_target_pairs={{0,16},{8,24},{16,0},{24,8},{1,17},{9,25},{17,1},{25,9},{2,18},{10... | collective-permute-start | bytes 3145736 | tf_op jit(solution)/shard_map/ppermute | solution.py:63
  452.9 237.9 %collective-permute-start.5 = (bf16[256,2048]{1,0:T(8,128)(2,1)}, bf16[256,2048]{1,0:T(8,128)(2,1)}, u32[]{:S(2)}, u32[]{:S(2)}) collective-permute-start(bf16[256,2048]{1,0:T(8,128)(2,1)} %fusion.86), channel_id=1, source_target_pairs={{0,24},{8,16},{16,8},{24,0},{1,25},{9,17},{17,9},{25,1},{2,26},{10... | collective-permute-start | bytes 3145736 | tf_op jit(solution)/shard_map/ppermute | solution.py:63
  456.0 237.0 %collective-permute-start.10 = (bf16[960,2048]{1,0:T(8,128)(2,1)}, bf16[960,2048]{1,0:T(8,128)(2,1)}, u32[]{:S(2)}, u32[]{:S(2)}) collective-permute-start(bf16[960,2048]{1,0:T(8,128)(2,1)} %get-tuple-element.797), channel_id=1, source_target_pairs={{0,1},{1,0},{2,3},{3,2},{4,5},{5,4},{6,7},{7,6},{8,9},{9,8},{10,11... | collective-permute-start | bytes 11796488 | tf_op jit(solution)/shard_map/ppermute | solution.py:63
  457.2 237.1 %collective-permute-start.11 = (bf16[960,2048]{1,0:T(8,128)(2,1)}, bf16[960,2048]{1,0:T(8,128)(2,1)}, u32[]{:S(2)}, u32[]{:S(2)}) collective-permute-start(bf16[960,2048]{1,0:T(8,128)(2,1)} %get-tuple-element.796), channel_id=1, source_target_pairs={{0,2},{1,3},{2,0},{3,1},{4,6},{5,7},{6,4},{7,5},{8,10},{9,11},{10,... | collective-permute-start | bytes 11796488 | tf_op jit(solution)/shard_map/ppermute | solution.py:63
  689.5 5.9 collective-permute-start
  690.0 47.4 %collective-permute-start.1 = (bf16[256,4096]{1,0:T(8,128)(2,1)}, bf16[256,4096]{1,0:T(8,128)(2,1)}, u32[]{:S(2)}, u32[]{:S(2)}) collective-permute-start(bf16[256,4096]{1,0:T(8,128)(2,1)} %get-tuple-element.801), channel_id=1, source_target_pairs={{0,16},{8,24},{16,0},{24,8},{1,17},{9,25},{17,1},{25,9},{2,18},{10... | collective-permute-start | bytes 6291464 | tf_op jit(solution)/shard_map/ppermute | solution.py:63
  690.8 92.1 %collective-permute-start.2 = (bf16[256,4096]{1,0:T(8,128)(2,1)}, bf16[256,4096]{1,0:T(8,128)(2,1)}, u32[]{:S(2)}, u32[]{:S(2)}) collective-permute-start(bf16[256,4096]{1,0:T(8,128)(2,1)} %get-tuple-element.800), channel_id=1, source_target_pairs={{0,24},{8,16},{16,8},{24,0},{1,25},{9,17},{17,9},{25,1},{2,26},{10... | collective-permute-start | bytes 6291464 | tf_op jit(solution)/shard_map/ppermute | solution.py:63
  693.0 509.2 %collective-permute-start.12 = (bf16[960,2048]{1,0:T(8,128)(2,1)}, bf16[960,2048]{1,0:T(8,128)(2,1)}, u32[]{:S(2)}, u32[]{:S(2)}) collective-permute-start(bf16[960,2048]{1,0:T(8,128)(2,1)} %get-tuple-element.795), channel_id=1, source_target_pairs={{0,3},{1,2},{2,1},{3,0},{4,7},{5,6},{6,5},{7,4},{8,11},{9,10},{10,... | collective-permute-start | bytes 11796488 | tf_op jit(solution)/shard_map/ppermute | solution.py:63
  694.3 513.2 %collective-permute-start.13 = (bf16[960,2048]{1,0:T(8,128)(2,1)}, bf16[960,2048]{1,0:T(8,128)(2,1)}, u32[]{:S(2)}, u32[]{:S(2)}) collective-permute-start(bf16[960,2048]{1,0:T(8,128)(2,1)} %get-tuple-element.794), channel_id=1, source_target_pairs={{0,4},{1,5},{2,6},{3,7},{4,0},{5,1},{6,2},{7,3},{8,12},{9,13},{10,... | collective-permute-start | bytes 11796488 | tf_op jit(solution)/shard_map/ppermute | solution.py:63
  695.4 548.3 %collective-permute-start.14 = (bf16[960,2048]{1,0:T(8,128)(2,1)}, bf16[960,2048]{1,0:T(8,128)(2,1)}, u32[]{:S(2)}, u32[]{:S(2)}) collective-permute-start(bf16[960,2048]{1,0:T(8,128)(2,1)} %get-tuple-element.793), channel_id=1, source_target_pairs={{0,5},{1,4},{2,7},{3,6},{4,1},{5,0},{6,3},{7,2},{8,13},{9,12},{10,... | collective-permute-start | bytes 11796488 | tf_op jit(solution)/shard_map/ppermute | solution.py:63
  737.4 592.9 %collective-permute-start.15 = (bf16[960,2048]{1,0:T(8,128)(2,1)}, bf16[960,2048]{1,0:T(8,128)(2,1)}, u32[]{:S(2)}, u32[]{:S(2)}) collective-permute-start(bf16[960,2048]{1,0:T(8,128)(2,1)} %get-tuple-element.798), channel_id=1, source_target_pairs={{0,6},{1,7},{2,4},{3,5},{4,2},{5,3},{6,0},{7,1},{8,14},{9,15},{10,... | collective-permute-start | bytes 11796488 | tf_op jit(solution)/shard_map/ppermute | solution.py:63
  782.9 632.5 %collective-permute-start.16 = (bf16[960,2048]{1,0:T(8,128)(2,1)}, bf16[960,2048]{1,0:T(8,128)(2,1)}, u32[]{:S(2)}, u32[]{:S(2)}) collective-permute-start(bf16[960,2048]{1,0:T(8,128)(2,1)} %get-tuple-element.792), channel_id=1, source_target_pairs={{0,7},{1,6},{2,5},{3,4},{4,3},{5,2},{6,1},{7,0},{8,15},{9,14},{10,... | collective-permute-start | bytes 11796488 | tf_op jit(solution)/shard_map/ppermute | solution.py:63
  1175.4 11.0 copy-start.3
Sparse Core Ops, SparseCore 0:
  20.0 205.7 all-reduce.1
Sparse Core Ops, SparseCore 1:
  73.6 120.8 all-gather.2
  683.2 492.1 all-gather.4
